TPU v7x, 32 devices: a whole 2x2x4 slice. The times are simulated.
32 devices in a mesh: dp: 2 (over core), seq: 4 (over z), head: 4 (over y, x).
Axes of the slice: x: 2, y: 2, z: 4, core: 2. Of those that a mesh axis runs over, the one named last changes fastest.
Arguments:
- x_in: float32 [2, 512, 1024], P('dp', 'seq'), may hold values from -6 to 6
- cotangent: float32 [2, 512, 1024], P('dp', 'seq'), may hold values from -6 to 6
- attn_gain: bfloat16 [1024], P('seq'), may hold values from 0.25 to 1.75
- w_query: bfloat16 [1024, 512], P('seq', 'head'), may hold values from -0.1875 to 0.1875
- w_key: bfloat16 [1024, 512], P('seq', 'head'), may hold values from -0.1875 to 0.1875
- w_value: bfloat16 [1024, 1024], P('seq', 'head'), may hold values from -0.1875 to 0.1875
- w_outgate: bfloat16 [1024, 1024], P('seq', 'head'), may hold values from -0.1875 to 0.1875
- w_lowrank: bfloat16 [1024, 16], P('seq'), may hold values from -0.1875 to 0.1875
- w_forget: float32 [16, 512], replicated, may hold values from -1.5 to 1.5
- forget_bias: float32 [512], replicated, may hold values from -1 to 6
- group_gain: float32 [256], replicated, may hold values from 0.25 to 1.75
- w_output: bfloat16 [1024, 1024], P('head', 'seq'), may hold values from -0.375 to 0.375
- mlp_gain: bfloat16 [1024], P('seq'), may hold values from 0.25 to 1.75
- w_gate: bfloat16 [1024, 2816], P('seq', 'head'), may hold values from -0.1875 to 0.1875
- w_up: bfloat16 [1024, 2816], P('seq', 'head'), may hold values from -0.1875 to 0.1875
- w_down: bfloat16 [2816, 1024], P('head', 'seq'), may hold values from -0.109375 to 0.109375
Outputs:
- block_out: float32 [2, 512, 1024], P('dp', 'seq')
- grad_input: float32 [2, 512, 1024], P('dp', 'seq')
- grad_attn_gain: float32 [1024], P('seq')
- grad_query: float32 [1024, 512], P('seq', 'head')
- grad_key: float32 [1024, 512], P('seq', 'head')
- grad_value: float32 [1024, 1024], P('seq', 'head')
- grad_outgate: float32 [1024, 1024], P('seq', 'head')
- grad_lowrank: float32 [1024, 16], P('seq')
- grad_forget: float32 [16, 512], replicated
- grad_bias: float32 [512], replicated
- grad_group_gain: float32 [256], replicated
- grad_output: float32 [1024, 1024], P('head', 'seq')
- grad_mlp_gain: float32 [1024], P('seq')
- grad_gate: float32 [1024, 2816], P('seq', 'head')
- grad_up: float32 [1024, 2816], P('seq', 'head')
- grad_down: float32 [2816, 1024], P('head', 'seq')
All inputs are finite; a program needn't handle non-finite values.
Results may differ from a plain program's by a relative error of at most 0.0097.
Values may be sent and summed in bfloat16 or wider, within the bound.
A program may use at most 128 MiB of HBM per device.

v0:
```python
import jax
import jax.numpy as jnp
from jax import lax
from jax.sharding import PartitionSpec as P

DK = 128
DV = 256
SPAN = 64
epsilon = 1e-06
normalizer = 16.0
highest = lax.Precision.HIGHEST


def entering(part, axis, combine, identity, reverse):
    count = lax.axis_size(axis)
    place = lax.axis_index(axis)
    ahead = count - 1 - place if reverse else place
    gathered = jax.tree.map(lambda a: lax.all_gather(a, axis), part)
    state = jax.tree.map(lambda a, e: jnp.zeros_like(a) + jnp.asarray(e, a.dtype), part, identity)

    def one(step, state):
        source = count - 1 - step if reverse else step
        return combine(
            state, jax.tree.map(lambda a: lax.dynamic_index_in_dim(a, source, 0, False), gathered)
        )

    return lax.fori_loop(0, ahead, one, state)


def product(left, right):
    return jnp.dot(left, right, preferred_element_type=jnp.float32)


def rms_rows(inputs):
    return lax.rsqrt(jnp.mean(inputs * inputs, axis=-1, keepdims=True) + epsilon)


def norm_back(inputs, scale, gain, grad):
    scaled = gain * grad
    gain_terms = grad * inputs * scale
    input_grad = scale * scaled - inputs * scale**3 * jnp.mean(
        scaled * inputs, axis=-1, keepdims=True
    )
    return (gain_terms, input_grad)


def compose(earlier, later):
    return (earlier[0] * later[0], later[0][..., None] * earlier[1] + later[1])


def mixer_block(queries, keys_in, values_in, log_decay, start_state):
    block_len = min(SPAN, queries.shape[0])
    blocks = queries.shape[0] // block_len

    def cut(array):
        return array.reshape(blocks, block_len, array.shape[-1])

    lower = jnp.tril(jnp.ones((block_len, block_len), jnp.float32))

    def block_step(carried, pieces):
        query_blk, key_blk, value_blk, decay_blk = pieces
        running = jnp.cumsum(decay_blk, axis=0)
        from_state = jnp.dot(query_blk * jnp.exp(running), carried, precision=highest)
        spread = (
            jnp.exp(jnp.minimum(running[:, None, :] - running[None, :, :], 0.0)) * lower[:, :, None]
        )
        scores = jnp.einsum("id,jd,ijd->ij", query_blk, key_blk, spread, precision=highest)
        inside = jnp.dot(scores, value_blk, precision=highest)
        ending = running[-1]
        weighted = key_blk * jnp.exp(ending[None, :] - running)
        carried = jnp.exp(ending)[:, None] * carried + jnp.dot(
            weighted.T, value_blk, precision=highest
        )
        return (carried, from_state + inside)

    final_state, outputs = lax.scan(
        jax.checkpoint(block_step),
        start_state,
        (cut(queries), cut(keys_in), cut(values_in), cut(log_decay)),
    )
    return (outputs.reshape(queries.shape[0], values_in.shape[-1]), final_state)


def on_device(
    x_in,
    cotangent,
    attn_gain,
    w_query,
    w_key,
    w_value,
    w_outgate,
    w_lowrank,
    w_forget,
    forget_bias,
    group_gain,
    w_output,
    mlp_gain,
    w_gate,
    w_up,
    w_down,
):
    (
        gain_one,
        wq_full,
        wk_full,
        wv_full,
        wg_full,
        wl_full,
        wo_full,
        gain_two,
        wgate_full,
        wup_full,
        wdown_full,
    ) = (
        lax.all_gather(attn_gain, "seq", axis=0, tiled=True),
        lax.all_gather(w_query, "seq", axis=0, tiled=True),
        lax.all_gather(w_key, "seq", axis=0, tiled=True),
        lax.all_gather(w_value, "seq", axis=0, tiled=True),
        lax.all_gather(w_outgate, "seq", axis=0, tiled=True),
        lax.all_gather(w_lowrank, "seq", axis=0, tiled=True),
        lax.all_gather(w_output, "seq", axis=1, tiled=True),
        lax.all_gather(mlp_gain, "seq", axis=0, tiled=True),
        lax.all_gather(w_gate, "seq", axis=0, tiled=True),
        lax.all_gather(w_up, "seq", axis=0, tiled=True),
        lax.all_gather(w_down, "seq", axis=1, tiled=True),
    )
    seqs_here, tok_here, width = x_in.shape
    total_rows = seqs_here * tok_here
    heads_here = wq_full.shape[1] // DK
    key_cols = heads_here * DK
    head_scale = DK ** (-0.5)
    head_pos = lax.axis_index("head")
    forget_cols = lax.dynamic_slice_in_dim(w_forget, head_pos * key_cols, key_cols, 1)
    bias_cols = lax.dynamic_slice_in_dim(forget_bias, head_pos * key_cols, key_cols, 0)
    gain_first = gain_one.astype(jnp.float32)
    gain_second = gain_two.astype(jnp.float32)

    def heads_of(array, size):
        return array.reshape(seqs_here, tok_here, heads_here, size).transpose(0, 2, 1, 3)

    def rows_of(array):
        return array.transpose(0, 2, 1, 3).reshape(total_rows, -1)

    flat_in = x_in.reshape(total_rows, width)
    flat_cot = cotangent.reshape(total_rows, width)
    scale_one = rms_rows(flat_in)
    normed_in = (flat_in * scale_one * gain_first).astype(jnp.bfloat16)
    q_rows = product(normed_in, wq_full)
    k_rows = product(normed_in, wk_full)
    v_rows = product(normed_in, wv_full)
    og_rows = product(normed_in, wg_full)
    low_rank = product(normed_in, wl_full)
    pre_gate = jnp.dot(low_rank, forget_cols, precision=highest) + bias_cols
    log_decay = jax.nn.log_sigmoid(pre_gate) / normalizer
    q_heads = heads_of(q_rows, DK)
    k_heads = heads_of(k_rows, DK)
    v_heads = heads_of(v_rows, DV)
    decay_heads = heads_of(log_decay, DK)
    running = jnp.cumsum(decay_heads, axis=2)
    ending = running[:, :, -1, :]
    decay_total = jnp.exp(ending)
    local_state = jnp.einsum(
        "shld,shlv->shdv",
        k_heads * jnp.exp(ending[:, :, None, :] - running),
        v_heads,
        precision=highest,
    )
    identity = (jnp.ones_like(decay_total), jnp.zeros_like(local_state))
    start_total, start_state = entering((decay_total, local_state), "seq", compose, identity, False)

    def mixed(q_part, k_part, v_part, d_part):
        return jax.vmap(jax.vmap(mixer_block))(
            q_part * head_scale, k_part, v_part, d_part, start_state
        )

    (o_heads, end_state), pullback = jax.vjp(mixed, q_heads, k_heads, v_heads, decay_heads)
    gate_heads = heads_of(og_rows, DV)
    scale_three = rms_rows(o_heads)
    gated_norm = o_heads * scale_three * group_gain
    gate_sig = jax.nn.sigmoid(gate_heads)
    gate_act = gate_heads * gate_sig
    mixed_out = rows_of(gated_norm * gate_act).astype(jnp.bfloat16)
    resid = flat_in + lax.psum(product(mixed_out, wo_full), "head")
    scale_two = rms_rows(resid)
    normed_mid = (resid * scale_two * gain_second).astype(jnp.bfloat16)
    gate_pre = product(normed_mid, wgate_full)
    up_pre = product(normed_mid, wup_full)
    gate_sigma = jax.nn.sigmoid(gate_pre)
    gate_silu = gate_pre * gate_sigma
    mlp_hidden = (gate_silu * up_pre).astype(jnp.bfloat16)
    result = resid + lax.psum(product(mlp_hidden, wdown_full).astype(jnp.bfloat16), "head").astype(
        jnp.float32
    )
    grad_out_b = flat_cot.astype(jnp.bfloat16)
    d_down = product(mlp_hidden.T, grad_out_b)
    d_hidden = product(grad_out_b, wdown_full.T)
    d_gate_pre = (d_hidden * up_pre * gate_sigma * (1.0 + gate_pre * (1.0 - gate_sigma))).astype(
        jnp.bfloat16
    )
    d_up_pre = (d_hidden * gate_silu).astype(jnp.bfloat16)
    d_gate = product(normed_mid.T, d_gate_pre)
    d_up = product(normed_mid.T, d_up_pre)
    d_normed_mid = lax.psum(
        product(d_gate_pre, wgate_full.T) + product(d_up_pre, wup_full.T), "head"
    )
    gain_terms, d_resid_norm = norm_back(resid, scale_two, gain_second, d_normed_mid)
    d_gain_two = jnp.sum(gain_terms, axis=0)
    d_resid = flat_cot + d_resid_norm
    d_resid_b = d_resid.astype(jnp.bfloat16)
    d_output = product(mixed_out.T, d_resid_b)
    d_mixed = heads_of(product(d_resid_b, wo_full.T), DV)
    d_norm_out = d_mixed * gate_act
    d_gate_heads = d_mixed * gated_norm * gate_sig * (1.0 + gate_heads * (1.0 - gate_sig))
    d_group = jnp.sum(d_norm_out * o_heads * scale_three, axis=(0, 1, 2))
    group_terms, d_o_heads = norm_back(o_heads, scale_three, group_gain, d_norm_out)
    state_grad = jnp.einsum(
        "shld,shlv->shdv", q_heads * head_scale * jnp.exp(running), d_o_heads, precision=highest
    )
    later_total, later_grad = entering((decay_total, state_grad), "seq", compose, identity, True)
    d_q, d_k, d_v, d_decay = pullback((d_o_heads, later_grad))
    d_pre = rows_of(d_decay) / normalizer * jax.nn.sigmoid(-pre_gate)
    d_bias = jnp.sum(d_pre, axis=0)
    d_forget = jnp.dot(low_rank.T, d_pre, precision=highest)
    d_low_part = jnp.dot(d_pre, forget_cols.T, precision=highest)
    d_q_b = rows_of(d_q).astype(jnp.bfloat16)
    d_k_b = rows_of(d_k).astype(jnp.bfloat16)
    d_v_b = rows_of(d_v).astype(jnp.bfloat16)
    d_og_b = rows_of(d_gate_heads).astype(jnp.bfloat16)
    d_query = product(normed_in.T, d_q_b)
    d_key = product(normed_in.T, d_k_b)
    d_value = product(normed_in.T, d_v_b)
    d_outgate = product(normed_in.T, d_og_b)
    d_in_part = (
        product(d_q_b, wq_full.T)
        + product(d_k_b, wk_full.T)
        + product(d_v_b, wv_full.T)
        + product(d_og_b, wg_full.T)
    )
    d_in_sum, d_low_sum = lax.psum((d_in_part, d_low_part), "head")
    d_low_b = d_low_sum.astype(jnp.bfloat16)
    d_lowrank = product(normed_in.T, d_low_b)
    d_normed_in = d_in_sum + product(d_low_b, wl_full.T)
    first_terms, d_in_norm = norm_back(flat_in, scale_one, gain_first, d_normed_in)
    d_gain_one = jnp.sum(first_terms, axis=0)
    grad_in = d_resid + d_in_norm
    parts = (
        lax.psum_scatter(d_gain_one, "seq", scatter_dimension=0, tiled=True),
        lax.psum_scatter(d_query, "seq", scatter_dimension=0, tiled=True),
        lax.psum_scatter(d_key, "seq", scatter_dimension=0, tiled=True),
        lax.psum_scatter(d_value, "seq", scatter_dimension=0, tiled=True),
        lax.psum_scatter(d_outgate, "seq", scatter_dimension=0, tiled=True),
        lax.psum_scatter(d_lowrank, "seq", scatter_dimension=0, tiled=True),
        lax.psum_scatter(d_output, "seq", scatter_dimension=1, tiled=True),
        lax.psum_scatter(d_gain_two, "seq", scatter_dimension=0, tiled=True),
        lax.psum_scatter(d_gate, "seq", scatter_dimension=0, tiled=True),
        lax.psum_scatter(d_up, "seq", scatter_dimension=0, tiled=True),
        lax.psum_scatter(d_down, "seq", scatter_dimension=1, tiled=True),
    )
    (
        s_gain_one,
        s_query,
        s_key,
        s_value,
        s_outgate,
        s_lowrank,
        s_output,
        s_gain_two,
        s_gate,
        s_up,
        s_down,
    ) = lax.psum(
        (
            parts[0],
            parts[1],
            parts[2],
            parts[3],
            parts[4],
            parts[5],
            parts[6],
            parts[7],
            parts[8],
            parts[9],
            parts[10],
        ),
        "dp",
    )
    forget_full = lax.dynamic_update_slice_in_dim(
        jnp.zeros(w_forget.shape, jnp.float32), d_forget, head_pos * key_cols, 1
    )
    bias_full = lax.dynamic_update_slice_in_dim(
        jnp.zeros(forget_bias.shape, jnp.float32), d_bias, head_pos * key_cols, 0
    )
    s_forget, s_bias, s_group = lax.psum((forget_full, bias_full, d_group), ("dp", "seq", "head"))
    return (
        result.reshape(seqs_here, tok_here, width),
        grad_in.reshape(seqs_here, tok_here, width),
        s_gain_one,
        s_query,
        s_key,
        s_value,
        s_outgate,
        s_lowrank,
        s_forget,
        s_bias,
        s_group,
        s_output,
        s_gain_two,
        s_gate,
        s_up,
        s_down,
    )


def solution(mesh):
    return jax.shard_map(
        on_device,
        mesh=mesh,
        in_specs=(
            P("dp", "seq", None),
            P("dp", "seq", None),
            P("seq"),
            P("seq", "head"),
            P("seq", "head"),
            P("seq", "head"),
            P("seq", "head"),
            P("seq", None),
            P(),
            P(),
            P(),
            P("head", "seq"),
            P("seq"),
            P("seq", "head"),
            P("seq", "head"),
            P("head", "seq"),
        ),
        out_specs=(
            P("dp", "seq", None),
            P("dp", "seq", None),
            P("seq"),
            P("seq", "head"),
            P("seq", "head"),
            P("seq", "head"),
            P("seq", "head"),
            P("seq", None),
            P(),
            P(),
            P(),
            P("head", "seq"),
            P("seq"),
            P("seq", "head"),
            P("seq", "head"),
            P("head", "seq"),
        ),
        check_vma=False,
    )
```

profile of v0, /device:TPU:0, one launch (start us, length us, event | category | flops | bytes accessed | tf_op | source)
XLA Modules:
  0.0 774.9 jit_solution(1150083508637122755)
XLA Ops:
  8.1 1.2 fusion.75
  10.6 12.6 %all-gather.2 = bf16[4,1,256]{2,1,0:T(2,128)(2,1)S(1)} all-gather(bf16[1,1,256]{2,1,0:T(2,128)(2,1)S(1)} %reshape.777), channel_id=1, replica_groups=mesh['dp'=2,'seq'=4,'head'=4] {'seq'}, dimensions={0}, use_global_device_ids=true | all-gather | bytes 2560 | tf_op jit(solution)/shard_map/all_gather | solution.py:115
  23.2 13.3 %all_gather.52 = bf16[1024,16]{0,1:T(8,128)(2,1)S(1)} all-gather(bf16[256,16]{0,1:T(8,128)(2,1)} %param.31), channel_id=1, replica_groups=mesh['dp'=2,'seq'=4,'head'=4] {'seq'}, dimensions={0}, use_global_device_ids=true | all-gather | bytes 40960 | tf_op jit(solution)/shard_map/all_gather | solution.py:120
  37.3 1.2 fusion.77
  39.2 15.9 %all_gather.55 = bf16[1024,256]{1,0:T(8,128)(2,1)S(1)} all-gather(bf16[256,256]{1,0:T(8,128)(2,1)S(1)} %copy-done.37), channel_id=1, replica_groups=mesh['dp'=2,'seq'=4,'head'=4] {'seq'}, dimensions={0}, use_global_device_ids=true | all-gather | bytes 655360 | tf_op jit(solution)/shard_map/all_gather | solution.py:118
  55.4 14.5 %all_gather.54 = bf16[1024,128]{1,0:T(8,128)(2,1)S(1)} all-gather(bf16[256,128]{1,0:T(8,128)(2,1)S(1)} %copy-done.41), channel_id=1, replica_groups=mesh['dp'=2,'seq'=4,'head'=4] {'seq'}, dimensions={0}, use_global_device_ids=true | all-gather | bytes 327680 | tf_op jit(solution)/shard_map/all_gather | solution.py:117
  70.5 15.0 %all-gather = f32[512,256]{1,0:T(8,128)S(1)} all-gather(f32[128,256]{1,0:T(8,128)S(1)} %fusion.104), channel_id=2, replica_groups=mesh['dp'=2,'seq'=4,'head'=4] {'seq'}, dimensions={0}, use_global_device_ids=true | all-gather | bytes 655360 | tf_op jit(solution)/shard_map/all_gather | solution.py:18
  85.5 8.7 %all_gather.53 = f32[4,1,1,128]{3,2,1,0:T(1,128)S(1)} all-gather(f32[1,1,1,128]{3,2,1,0:T(1,128)S(1)} %get-tuple-element.745), channel_id=1, replica_groups=mesh['dp'=2,'seq'=4,'head'=4] {'seq'}, dimensions={0}, use_global_device_ids=true | all-gather | bytes 2560 | tf_op jit(solution)/shard_map/all_gather | solution.py:18
  94.2 14.6 %all_gather.58 = bf16[1024,128]{1,0:T(8,128)(2,1)S(1)} all-gather(bf16[256,128]{1,0:T(8,128)(2,1)S(1)} %copy-done.42), channel_id=1, replica_groups=mesh['dp'=2,'seq'=4,'head'=4] {'seq'}, dimensions={0}, use_global_device_ids=true | all-gather | bytes 327680 | tf_op jit(solution)/shard_map/all_gather | solution.py:116
  109.6 6.8 while.70
  110.3 1.7 fusion.282
  113.7 1.7 fusion.282
  117.1 15.5 %all_gather.59 = bf16[1024,256]{1,0:T(8,128)(2,1)S(1)} all-gather(bf16[256,256]{1,0:T(8,128)(2,1)S(1)} %copy-done.38), channel_id=1, replica_groups=mesh['dp'=2,'seq'=4,'head'=4] {'seq'}, dimensions={0}, use_global_device_ids=true | all-gather | bytes 655360 | tf_op jit(solution)/shard_map/all_gather | solution.py:119
  132.6 14.8 %all_gather.60 = bf16[256,1024]{1,0:T(8,128)(2,1)S(1)} all-gather(bf16[256,256]{1,0:T(8,128)(2,1)S(1)} %copy-done.39), channel_id=1, replica_groups=mesh['dp'=2,'seq'=4,'head'=4] {'seq'}, dimensions={1}, use_global_device_ids=true | all-gather | bytes 655360 | tf_op jit(solution)/shard_map/all_gather | solution.py:121
  151.2 8.8 %all-gather.3 = bf16[4,1,256]{2,1,0:T(2,128)(2,1)S(1)} all-gather(bf16[1,1,256]{2,1,0:T(2,128)(2,1)S(1)} %reshape.779), channel_id=1, replica_groups=mesh['dp'=2,'seq'=4,'head'=4] {'seq'}, dimensions={0}, use_global_device_ids=true | all-gather | bytes 2560 | tf_op jit(solution)/shard_map/all_gather | solution.py:122
  161.1 32.6 %all-reduce.13.cloned.1.call-done = f32[128,1024]{1,0:T(8,128)} async-done(((f32[128,1024]{1,0:T(8,128)}), f32[128,1024]{1,0:T(8,128)}) %all-reduce.13.cloned.1.call-update) | async-done | bytes 524304 | tf_op jit(solution)/shard_map/psum | solution.py:183
  193.7 1.2 multiply_reduce_fusion.3
  195.6 2.7 fusion.132
  198.3 22.5 %all-gather.10.cloned.1.call-done = bf16[1024,704]{0,1:T(8,128)(2,1)} async-done(((bf16[256,704]{0,1:T(8,128)(2,1)}), bf16[1024,704]{0,1:T(8,128)(2,1)}) %all-gather.10.cloned.1.call-update) | async-done | bytes 1441808 | tf_op jit(solution)/shard_map/all_gather | solution.py:124
  220.8 2.6 fusion.133
  223.4 32.5 %all-gather.12.cloned.1.call-done = bf16[704,1024]{1,0:T(8,128)(2,1)} async-done(((bf16[704,256]{1,0:T(8,128)(2,1)}), bf16[704,1024]{1,0:T(8,128)(2,1)}) %all-gather.12.cloned.1.call-update) | async-done | bytes 1441808 | tf_op jit(solution)/shard_map/all_gather | solution.py:125
  255.9 2.2 multiply_convert_fusion.2
  258.8 1.2 convolution_add_fusion.2
  260.9 2.5 convolution_convert_fusion
  263.4 40.4 %all-reduce.17.cloned.1.call-done = f32[128,1024]{1,0:T(8,128)} async-done(((f32[128,1024]{1,0:T(8,128)}), f32[128,1024]{1,0:T(8,128)}) %all-reduce.17.cloned.1.call-update) | async-done | bytes 524304 | tf_op jit(solution)/shard_map/psum | solution.py:203
  303.8 1.8 multiply_reduce_fusion.1
  305.6 44.8 %all-reduce.15.cloned.1.call-done = bf16[128,1024]{1,0:T(8,128)(2,1)} async-done(((bf16[128,1024]{1,0:T(8,128)(2,1)}), bf16[128,1024]{1,0:T(8,128)(2,1)}) %all-reduce.15.cloned.1.call-update) | async-done | bytes 262160 | tf_op jit(solution)/shard_map/psum | solution.py:191
  350.4 2.3 bitcast_add_fusion.7
  352.7 2.6 fusion.94
  355.7 15.3 %all-gather.1 = f32[512,256]{1,0:T(8,128)S(1)} all-gather(f32[128,256]{1,0:T(8,128)S(1)} %fusion.107), channel_id=3, replica_groups=mesh['dp'=2,'seq'=4,'head'=4] {'seq'}, dimensions={0}, use_global_device_ids=true | all-gather | bytes 655360 | tf_op jit(solution)/shard_map/all_gather | solution.py:18
  371.0 2.6 while.69
  374.3 19.5 %while.71 = (s32[]{:T(128)}, f32[1,1,128,256]{2,3,1,0:T(8,128)S(1)}, f32[2,1,1,64,128]{4,3,2,1,0:T(8,128)S(1)}, bf16[2,1,1,64,128]{4,3,2,1,0:T(8,128)(2,1)}, bf1...) while((s32[]{:T(128)}, ...), condition=%wide.region_23.24_spmd.clone.clone, body=%wide.region_16.23_spmd.clone.sunk.clone | while | flops 141848576 | bytes 4776213 | solution.py:76
  376.6 1.3 fusion.300
  378.0 1.2 fusion.298
  379.7 2.3 fusion.303
  386.3 1.3 fusion.300
  387.8 1.2 fusion.298
  389.4 2.3 fusion.303
  394.7 1.1 fusion.136
  395.8 1.8 fusion.137
  397.7 1.4 fusion.95
  399.2 1.3 fusion.138
  400.6 1.3 fusion.139
  402.0 2.1 fusion.140
  405.0 2.1 fusion.141
  408.2 2.2 fusion.124
  412.1 1.1 convolution_add_fusion.5
  413.6 9.2 %psum.137 = bf16[128,16]{0,1:T(8,128)(2,1)S(1)} all-reduce(f32[128,16]{0,1:T(8,128)S(1)} %fusion.111), channel_id=1, replica_groups=mesh['dp'=2,'seq'=4,'head'=4] {'head'}, use_global_device_ids=true, to_apply=%region_25.26 | all-reduce | flops 2048 | bytes 12288 | tf_op jit(solution)/shard_map/psum | solution.py:239
  423.7 15.4 %reduce-scatter.12.cloned.1.call-done = f32[256,128]{1,0:T(8,128)} async-done(((f32[1024,128]{1,0:T(8,128)}), f32[256,128]{1,0:T(8,128)}) %reduce-scatter.12.cloned.1.call-update) | async-done | bytes 131088 | tf_op jit(solution)/shard_map/reduce_scatter | solution.py:249
  439.2 27.9 %reduce-scatter.20.cloned.1.call-done = f32[256,256]{1,0:T(8,128)} async-done(((f32[256,1024]{1,0:T(8,128)}), f32[256,256]{1,0:T(8,128)}) %reduce-scatter.20.cloned.1.call-update) | async-done | bytes 262160 | tf_op jit(solution)/shard_map/reduce_scatter | solution.py:253
  467.1 27.9 %reduce-scatter.14.cloned.1.call-done = f32[256,256]{1,0:T(8,128)} async-done(((f32[1024,256]{1,0:T(8,128)}), f32[256,256]{1,0:T(8,128)}) %reduce-scatter.14.cloned.1.call-update) | async-done | bytes 262160 | tf_op jit(solution)/shard_map/reduce_scatter | solution.py:250
  495.0 27.9 %reduce-scatter.16.cloned.1.call-done = f32[256,256]{1,0:T(8,128)} async-done(((f32[1024,256]{1,0:T(8,128)}), f32[256,256]{1,0:T(8,128)}) %reduce-scatter.16.cloned.1.call-update) | async-done | bytes 262160 | tf_op jit(solution)/shard_map/reduce_scatter | solution.py:251
  522.9 57.0 %reduce-scatter.22.cloned.1.call-done = f32[256,704]{0,1:T(8,128)} async-done(((f32[1024,704]{0,1:T(8,128)}), f32[256,704]{0,1:T(8,128)}) %reduce-scatter.22.cloned.1.call-update) | async-done | bytes 720912 | tf_op jit(solution)/shard_map/reduce_scatter | solution.py:255
  579.9 58.4 %reduce-scatter.24.cloned.1.call-done = f32[256,704]{0,1:T(8,128)} async-done(((f32[1024,704]{0,1:T(8,128)}), f32[256,704]{0,1:T(8,128)}) %reduce-scatter.24.cloned.1.call-update) | async-done | bytes 720912 | tf_op jit(solution)/shard_map/reduce_scatter | solution.py:256
  638.2 58.2 %reduce-scatter.26.cloned.1.call-done = f32[704,256]{1,0:T(8,128)} async-done(((f32[704,1024]{1,0:T(8,128)}), f32[704,256]{1,0:T(8,128)}) %reduce-scatter.26.cloned.1.call-update) | async-done | bytes 720912 | tf_op jit(solution)/shard_map/reduce_scatter | solution.py:257
  698.2 40.7 %all-reduce.3 = (f32[16,512]{1,0:T(8,128)}, f32[512]{0:T(512)}, f32[256]{0:T(256)}) all-reduce(f32[16,512]{1,0:T(8,128)S(1)} %convolution_dynamic-update-slice_fusion, f32[512]{0:T(512)S(1)} %dynamic_update_slice.52, f32[256]{0:T(256)S(1)} %copy-done.48), channel_id=1, replica_groups=mesh['dp'=2,'seq'=4,'head'=4] {'dp','seq','head'}, use_global_device_ids=true, to_apply=%region_40.41 | all-reduce | flops 8960 | bytes 71680 | tf_op jit(solution)/shard_map/psum | solution.py:293
  738.9 1.4 fusion.84
  740.3 10.8 %all-reduce.4 = (f32[1024]{0:T(1024)S(1)}, f32[1024]{0:T(1024)S(1)}) all-reduce(f32[1024]{0:T(1024)S(1)} %get-tuple-element.643, f32[1024]{0:T(1024)S(1)} %copy-done.43), channel_id=4, replica_groups=mesh['dp'=2,'seq'=4,'head'=4] {'seq'}, use_global_device_ids=true, to_apply=%region_28.29.clone | all-reduce | flops 2048 | bytes 16384
  751.3 4.6 all-reduce.5
  756.9 1.7 copy.186
  758.5 1.6 copy.187
  760.1 1.7 copy.188
  761.9 1.7 copy.189
  763.5 1.7 copy.190
  (285 shorter events, 39.0 us)
Async XLA Ops:
  8.0 30.6 %copy-start = (f32[16,512]{1,0:T(8,128)S(1)}, f32[16,512]{1,0:T(8,128)}, u32[]{:S(2)}) copy-start(f32[16,512]{1,0:T(8,128)} %param.32) | copy-start | bytes 98308
  8.0 31.2 %copy-start.37 = (bf16[256,256]{1,0:T(8,128)(2,1)S(1)}, bf16[256,256]{1,0:T(8,128)(2,1)}, u32[]{:S(2)}) copy-start(bf16[256,256]{1,0:T(8,128)(2,1)} %param.29) | copy-start | bytes 393220
  8.0 47.3 %copy-start.41 = (bf16[256,128]{1,0:T(8,128)(2,1)S(1)}, bf16[256,128]{1,0:T(8,128)(2,1)}, u32[]{:S(2)}) copy-start(bf16[256,128]{1,0:T(8,128)(2,1)} %param.28) | copy-start | bytes 196612
  8.0 185.7 %all-reduce.13.cloned.1.call-start = ((), (), s32[]{:S(2)}) async-start(), calls=%async_computation.9 | async-start | bytes 1048576 | tf_op jit(solution)/shard_map/psum | solution.py:183
  9.9 250.8 %copy-start.44 = (f32[128]{0:T(128)}, f32[128]{0:T(128)S(1)}, u32[]{:S(2)}) copy-start(f32[128]{0:T(128)S(1)} %get-tuple-element.747) | copy-start | bytes 1540
  39.0 55.2 %copy-start.24 = (f32[128,128]{1,0:T(8,128)}, f32[128,128]{1,0:T(8,128)S(1)}, u32[]{:S(2)}) copy-start(f32[128,128]{1,0:T(8,128)S(1)} %convolution_add_fusion.7) | copy-start | bytes 196612
  55.4 38.8 %copy-start.42 = (bf16[256,128]{1,0:T(8,128)(2,1)S(1)}, bf16[256,128]{1,0:T(8,128)(2,1)}, u32[]{:S(2)}) copy-start(bf16[256,128]{1,0:T(8,128)(2,1)} %param.27) | copy-start | bytes 196612
  69.9 24.3 %copy-start.7 = (bf16[1024,128]{1,0:T(8,128)(2,1)}, bf16[1024,128]{1,0:T(8,128)(2,1)S(1)}, u32[]{:S(2)}) copy-start(bf16[1024,128]{1,0:T(8,128)(2,1)S(1)} %all_gather.54) | copy-start | bytes 786436
  94.2 15.3 %copy-start.46 = (f32[4,1,1,128]{3,2,1,0:T(1,128)}, f32[4,1,1,128]{3,2,1,0:T(1,128)S(1)}, u32[]{:S(2)}) copy-start(f32[4,1,1,128]{3,2,1,0:T(1,128)S(1)} %get-tuple-element.1287) | copy-start | bytes 6148
  109.1 8.0 %copy-start.38 = (bf16[256,256]{1,0:T(8,128)(2,1)S(1)}, bf16[256,256]{1,0:T(8,128)(2,1)}, u32[]{:S(2)}) copy-start(bf16[256,256]{1,0:T(8,128)(2,1)} %param.30) | copy-start | bytes 393220
  109.1 23.5 %copy-start.39 = (bf16[256,256]{1,0:T(8,128)(2,1)S(1)}, bf16[256,256]{1,0:T(8,128)(2,1)}, u32[]{:S(2)}) copy-start(bf16[256,256]{1,0:T(8,128)(2,1)} %param.35) | copy-start | bytes 393220
  109.1 38.3 %copy-start.47 = (f32[256]{0:T(256)S(1)}, f32[256]{0:T(256)}, u32[]{:S(2)}) copy-start(f32[256]{0:T(256)} %param.34) | copy-start | bytes 3076
  116.4 33.0 %copy-start.29 = (f32[2,1,1,64,256]{4,3,2,1,0:T(8,128)}, f32[2,1,1,64,256]{4,3,2,1,0:T(8,128)S(1)}, u32[]{:S(2)}) copy-start(f32[2,1,1,64,256]{4,3,2,1,0:T(8,128)S(1)} %get-tuple-element.459) | copy-start | bytes 393220
  117.1 43.5 %copy-start.50 = (f32[128]{0:T(128)}, f32[128]{0:T(128)S(1)}, u32[]{:S(2)}) copy-start(f32[128]{0:T(128)S(1)} %rsqrt.38) | copy-start | bytes 1540
  132.6 17.9 %copy-start.9 = (bf16[1024,256]{1,0:T(8,128)(2,1)}, bf16[1024,256]{1,0:T(8,128)(2,1)S(1)}, u32[]{:S(2)}) copy-start(bf16[1024,256]{1,0:T(8,128)(2,1)S(1)} %all_gather.59) | copy-start | bytes 1572868
  147.4 47.5 %copy-start.11 = (bf16[256,1024]{1,0:T(8,128)(2,1)}, bf16[256,1024]{1,0:T(8,128)(2,1)S(1)}, u32[]{:S(2)}) copy-start(bf16[256,1024]{1,0:T(8,128)(2,1)S(1)} %all_gather.60) | copy-start | bytes 1572868
  147.4 3.8 copy-start.53
  147.4 46.3 %copy-start.1 = (f32[1,128,1024]{2,1,0:T(8,128)S(1)}, f32[1,128,1024]{2,1,0:T(8,128)}, u32[]{:S(2)}) copy-start(f32[1,128,1024]{2,1,0:T(8,128)} %param.24) | copy-start | bytes 1572868
  148.3 12.8 %copy-start.34 = (bf16[128,256]{1,0:T(8,128)(2,1)}, bf16[128,256]{1,0:T(8,128)(2,1)S(1)}, u32[]{:S(2)}) copy-start(bf16[128,256]{1,0:T(8,128)(2,1)S(1)} %get-tuple-element.750) | copy-start | bytes 196612
  149.4 46.2 %all-gather.8.cloned.1.call-start = ((), (), s32[]{:S(2)}) async-start(), calls=%async_computation.10 | async-start | bytes 1802240 | tf_op jit(solution)/shard_map/all_gather | solution.py:123
  149.9 70.9 %all-gather.10.cloned.1.call-start = ((), (), s32[]{:S(2)}) async-start(), calls=%async_computation.11 | async-start | bytes 1802240 | tf_op jit(solution)/shard_map/all_gather | solution.py:124
  150.5 105.4 %all-gather.12.cloned.1.call-start = ((), (), s32[]{:S(2)}) async-start(), calls=%async_computation.12 | async-start | bytes 1802240 | tf_op jit(solution)/shard_map/all_gather | solution.py:125
  151.1 152.7 %all-reduce.17.cloned.1.call-start = ((), (), s32[]{:S(2)}) async-start(), calls=%async_computation.14 | async-start | bytes 1048576 | tf_op jit(solution)/shard_map/psum | solution.py:203
  195.5 60.4 %copy-start.12 = (f32[1,128,1024]{2,1,0:T(8,128)S(1)}, f32[1,128,1024]{2,1,0:T(8,128)}, u32[]{:S(2)}) copy-start(f32[1,128,1024]{2,1,0:T(8,128)} %param.25) | copy-start | bytes 1572868
  255.9 2.3 copy-start.2
  255.9 2.9 copy-start.3
  258.2 1.9 copy-start.20
  258.2 2.7 copy-start.15
  260.1 90.3 %all-reduce.15.cloned.1.call-start = ((), (), s32[]{:S(2)}) async-start(), calls=%async_computation.13 | async-start | bytes 524288 | tf_op jit(solution)/shard_map/psum | solution.py:191
  263.3 89.4 %copy-start.30 = (f32[2,1,1,64,256]{4,3,2,1,0:T(8,128)S(1)}, f32[2,1,1,64,256]{4,3,2,1,0:T(8,128)}, u32[]{:S(2)}) copy-start(f32[2,1,1,64,256]{4,3,2,1,0:T(8,128)} %copy-done.29) | copy-start | bytes 393220
  263.3 89.4 %copy-start.51 = (f32[128]{0:T(128)S(1)}, f32[128]{0:T(128)}, u32[]{:S(2)}) copy-start(f32[128]{0:T(128)} %copy-done.50) | copy-start | bytes 1540
  263.4 160.4 %reduce-scatter.10.cloned.1.call-start = ((), (), s32[]{:S(2)}) async-start(), calls=%async_computation.16 | async-start | bytes 655360 | tf_op jit(solution)/shard_map/reduce_scatter | solution.py:248
  350.4 4.9 copy-start.40
  350.4 4.9 copy-start.52
  355.4 15.6 %copy-start.4 = (f32[128,256]{1,0:T(8,128)}, f32[128,256]{1,0:T(8,128)S(1)}, u32[]{:S(2)}) copy-start(f32[128,256]{1,0:T(8,128)S(1)} %fusion.91) | copy-start | bytes 393220
  374.3 5.0 copy-start.31
  376.6 6.6 copy-start.26
  379.6 4.3 copy-start.32
  384.1 5.0 copy-start.31
  386.3 6.6 copy-start.26
  389.3 4.3 copy-start.32
  393.8 3.9 copy-start.35
  395.8 3.4 copy-start.28
  395.8 43.4 %reduce-scatter.12.cloned.1.call-start = ((), (), s32[]{:S(2)}) async-start(), calls=%async_computation.17 | async-start | bytes 655360 | tf_op jit(solution)/shard_map/reduce_scatter | solution.py:249
  397.7 69.4 %reduce-scatter.20.cloned.1.call-start = ((), (), s32[]{:S(2)}) async-start(), calls=%async_computation.21 | async-start | bytes 1310720 | tf_op jit(solution)/shard_map/reduce_scatter | solution.py:253
  399.1 95.8 %reduce-scatter.14.cloned.1.call-start = ((), (), s32[]{:S(2)}) async-start(), calls=%async_computation.18 | async-start | bytes 1310720 | tf_op jit(solution)/shard_map/reduce_scatter | solution.py:250
  399.2 2.8 copy-start.21
  400.5 122.3 %reduce-scatter.16.cloned.1.call-start = ((), (), s32[]{:S(2)}) async-start(), calls=%async_computation.19 | async-start | bytes 1310720 | tf_op jit(solution)/shard_map/reduce_scatter | solution.py:251
  401.9 178.0 %reduce-scatter.22.cloned.1.call-start = ((), (), s32[]{:S(2)}) async-start(), calls=%async_computation.22 | async-start | bytes 3604480 | tf_op jit(solution)/shard_map/reduce_scatter | solution.py:255
  404.1 234.1 %reduce-scatter.24.cloned.1.call-start = ((), (), s32[]{:S(2)}) async-start(), calls=%async_computation.23 | async-start | bytes 3604480 | tf_op jit(solution)/shard_map/reduce_scatter | solution.py:256
  407.2 289.3 %reduce-scatter.26.cloned.1.call-start = ((), (), s32[]{:S(2)}) async-start(), calls=%async_computation.24 | async-start | bytes 3604480 | tf_op jit(solution)/shard_map/reduce_scatter | solution.py:257
  410.4 1.7 copy-start.10
  410.4 328.5 %all-reduce.19.cloned.1.call-start = ((), (), s32[]{:S(2)}) async-start(), calls=%async_computation.15 | async-start | bytes 1048576 | tf_op jit(solution)/shard_map/psum | solution.py:239
  411.8 1.5 copy-start.25
  413.3 283.2 %copy-start.54 = (u32[32]{0:T(128)S(1)}, u32[32]{0:T(128)}, u32[]{:S(2)}) copy-start(u32[32]{0:T(128)} %constant.207) | copy-start | bytes 388
  413.3 284.9 %copy-start.48 = (f32[256]{0:T(256)S(1)}, f32[256]{0:T(256)}, u32[]{:S(2)}) copy-start(f32[256]{0:T(256)} %get-tuple-element.645) | copy-start | bytes 3076
  413.3 325.6 %copy-start.45 = (f32[128]{0:T(128)S(1)}, f32[128]{0:T(128)}, u32[]{:S(2)}) copy-start(f32[128]{0:T(128)} %copy-done.44) | copy-start | bytes 1540
  413.3 338.0 %reduce-scatter.18.cloned.1.call-start = ((), (), s32[]{:S(2)}) async-start(), calls=%async_computation.20 | async-start | bytes 81920 | tf_op jit(solution)/shard_map/reduce_scatter | solution.py:252
  423.6 333.2 %all-reduce.21.cloned.1.call-start = ((), (), s32[]{:S(2)}) async-start(), calls=%async_computation.25 | async-start | bytes 6422528 | tf_op jit(solution)/shard_map/psum | solution.py:271
  696.5 43.9 %copy-start.43 = (f32[1024]{0:T(1024)S(1)}, f32[1024]{0:T(1024)}, u32[]{:S(2)}) copy-start(f32[1024]{0:T(1024)} %get-tuple-element.641) | copy-start | bytes 12292
  696.5 59.4 %copy-start.49 = (f32[128]{0:T(128)S(1)}, f32[128]{0:T(128)}, u32[]{:S(2)}) copy-start(f32[128]{0:T(128)} %get-tuple-element.746) | copy-start | bytes 1540
  756.9 8.3 %copy-start.19 = (f32[256,704]{0,1:T(8,128)S(1)}, f32[256,704]{0,1:T(8,128)}, u32[]{:S(2)}) copy-start(f32[256,704]{0,1:T(8,128)} %get-tuple-element.1182) | copy-start | bytes 2162692
  756.9 9.2 %copy-start.18 = (f32[256,704]{0,1:T(8,128)S(1)}, f32[256,704]{0,1:T(8,128)}, u32[]{:S(2)}) copy-start(f32[256,704]{0,1:T(8,128)} %get-tuple-element.1183) | copy-start | bytes 2162692
  760.1 6.8 copy-start.17
  (12 other events, 11.2 us)
Sparse Core Ops, SparseCore 0:
  149.5 44.1 all-reduce.12
  260.2 43.5 all-reduce.16
  307.3 43.0 all-reduce.14
  414.5 43.8 all-reduce.18
  696.6 23.7 all-reduce.20
Sparse Core Ops, SparseCore 1:
  151.4 34.3 all-gather.7
  187.1 33.6 all-gather.9
  222.2 33.6 all-gather.11
  395.8 20.2 reduce-scatter.9
  419.0 20.1 reduce-scatter.11
  441.5 25.5 reduce-scatter.19
  469.2 25.7 reduce-scatter.13
  497.1 25.7 reduce-scatter.15
  525.1 54.8 reduce-scatter.21
  582.2 56.0 reduce-scatter.23
  640.4 56.0 reduce-scatter.25
  699.3 18.9 reduce-scatter.17
where the time goes:
time: 776 us; the launch traced here: 775 us
  waiting for transfers between devices  447 us (58%)
  blocking collectives  214 us (28%)
  matrix products  40.4 us (5%)
  other arithmetic  28.8 us (4%)
  local copies, waits for them, and re-layouts  25.7 us (3%)
  between operations  16.7 us (2%)
    reduce_scatter x1, waiting for transfers between devices, on_device(): lax.psum_scatter(d_up, 'seq', scatter_dimension=0, tiled=True)  58.4 us
    reduce_scatter x1, waiting for transfers between devices, on_device(): lax.psum_scatter(d_down, 'seq', scatter_dimension=1, tiled=True)  58.2 us
    reduce_scatter x1, waiting for transfers between devices, on_device(): lax.psum_scatter(d_gate, 'seq', scatter_dimension=0, tiled=True)  57 us
    psum x1, waiting for transfers between devices, on_device(): lax.psum(product(mlp_hidden, wdown_full).astype(jnp.bfloat16), 'head')  44.8 us
    psum x1, blocking collectives, on_device(): lax.psum((forget_full, bias_full, d_group), ('dp', 'seq', 'head'))  40.7 us
    psum x1, waiting for transfers between devices, on_device(): lax.psum(product(d_gate_pre, wgate_full.T) + product(d_up_pre, wup_full.T...  40.4 us
    all_gather x3, blocking collectives, entering(): gathered = jax.tree.map(lambda a: lax.all_gather(a, axis), part)  39 us
    dot_general x27, matrix products, product(): return jnp.dot(left, right, preferred_element_type=jnp.float32)  34.3 us
  transfers between devices with their start and end apart: 17, of which 12 were waited for; matrix products, arithmetic and copies ran while one was open for 4% of the time, Pallas kernels for 0%

commit v1 on v0

--- a/solution.py
+++ b/solution.py
@@ -290,7 +290,9 @@
     bias_full = lax.dynamic_update_slice_in_dim(
         jnp.zeros(forget_bias.shape, jnp.float32), d_bias, head_pos * key_cols, 0
     )
-    s_forget, s_bias, s_group = lax.psum((forget_full, bias_full, d_group), ("dp", "seq", "head"))
+    s_forget, s_bias, s_group = lax.psum(
+        lax.psum((forget_full, bias_full, d_group), "dp"), ("seq", "head")
+    )
     return (
         result.reshape(seqs_here, tok_here, width),
         grad_in.reshape(seqs_here, tok_here, width),

time: 776 us -> 818 us (1.054)
  blocking collectives: 214 us -> 248 us
  waiting for transfers between devices: 447 us -> 456 us
    psum x1, blocking collectives: 40.7 us -> 74.5 us  [on_device(): lax.psum(lax.psum((forget_full, bias_full, d_group), 'dp'), ('seq', 'head'))]
  transfers between devices with their start and end apart: 17 -> 17, of which waited for: 12 -> 13; matrix products, arithmetic and copies ran while one was open for 4% -> 4% of each run, Pallas kernels for 0% -> 0%
where the time goes in v1:
time: 818 us; the launch traced here: 817 us
  waiting for transfers between devices  456 us (56%)
  blocking collectives  248 us (30%)
  matrix products  40.4 us (5%)
  other arithmetic  28.8 us (4%)
  local copies, waits for them, and re-layouts  25.7 us (3%)
  between operations  16.7 us (2%)
    psum x1, blocking collectives, on_device(): lax.psum(lax.psum((forget_full, bias_full, d_group), 'dp'), ('seq', 'head'))  74.5 us
    reduce_scatter x1, waiting for transfers between devices, on_device(): lax.psum_scatter(d_up, 'seq', scatter_dimension=0, tiled=True)  58.4 us
    reduce_scatter x1, waiting for transfers between devices, on_device(): lax.psum_scatter(d_down, 'seq', scatter_dimension=1, tiled=True)  58.2 us
    reduce_scatter x1, waiting for transfers between devices, on_device(): lax.psum_scatter(d_gate, 'seq', scatter_dimension=0, tiled=True)  57 us
    psum x1, waiting for transfers between devices, on_device(): lax.psum(product(mlp_hidden, wdown_full).astype(jnp.bfloat16), 'head')  44.8 us
    psum x1, waiting for transfers between devices, on_device(): lax.psum(product(d_gate_pre, wgate_full.T) + product(d_up_pre, wup_full.T...  40.4 us
    all_gather x3, blocking collectives, entering(): gathered = jax.tree.map(lambda a: lax.all_gather(a, axis), part)  39 us
    dot_general x27, matrix products, product(): return jnp.dot(left, right, preferred_element_type=jnp.float32)  34.3 us
  transfers between devices with their start and end apart: 17, of which 13 were waited for; matrix products, arithmetic and copies ran while one was open for 4% of the time, Pallas kernels for 0%

profile of v1, /device:TPU:0, one launch (start us, length us, event | category | flops | bytes accessed | tf_op | source)
XLA Modules:
  0.0 816.5 jit_solution(14429585581531067307)
XLA Ops:
  8.1 1.2 fusion.75
  10.6 12.6 %all-gather.2 = bf16[4,1,256]{2,1,0:T(2,128)(2,1)S(1)} all-gather(bf16[1,1,256]{2,1,0:T(2,128)(2,1)S(1)} %reshape.777), channel_id=1, replica_groups=mesh['dp'=2,'seq'=4,'head'=4] {'seq'}, dimensions={0}, use_global_device_ids=true | all-gather | bytes 2560 | tf_op jit(solution)/shard_map/all_gather | solution.py:115
  23.2 13.3 %all_gather.52 = bf16[1024,16]{0,1:T(8,128)(2,1)S(1)} all-gather(bf16[256,16]{0,1:T(8,128)(2,1)} %param.31), channel_id=1, replica_groups=mesh['dp'=2,'seq'=4,'head'=4] {'seq'}, dimensions={0}, use_global_device_ids=true | all-gather | bytes 40960 | tf_op jit(solution)/shard_map/all_gather | solution.py:120
  37.3 1.2 fusion.77
  39.2 15.9 %all_gather.55 = bf16[1024,256]{1,0:T(8,128)(2,1)S(1)} all-gather(bf16[256,256]{1,0:T(8,128)(2,1)S(1)} %copy-done.37), channel_id=1, replica_groups=mesh['dp'=2,'seq'=4,'head'=4] {'seq'}, dimensions={0}, use_global_device_ids=true | all-gather | bytes 655360 | tf_op jit(solution)/shard_map/all_gather | solution.py:118
  55.4 14.5 %all_gather.54 = bf16[1024,128]{1,0:T(8,128)(2,1)S(1)} all-gather(bf16[256,128]{1,0:T(8,128)(2,1)S(1)} %copy-done.41), channel_id=1, replica_groups=mesh['dp'=2,'seq'=4,'head'=4] {'seq'}, dimensions={0}, use_global_device_ids=true | all-gather | bytes 327680 | tf_op jit(solution)/shard_map/all_gather | solution.py:117
  70.5 15.0 %all-gather = f32[512,256]{1,0:T(8,128)S(1)} all-gather(f32[128,256]{1,0:T(8,128)S(1)} %fusion.104), channel_id=2, replica_groups=mesh['dp'=2,'seq'=4,'head'=4] {'seq'}, dimensions={0}, use_global_device_ids=true | all-gather | bytes 655360 | tf_op jit(solution)/shard_map/all_gather | solution.py:18
  85.5 8.7 %all_gather.53 = f32[4,1,1,128]{3,2,1,0:T(1,128)S(1)} all-gather(f32[1,1,1,128]{3,2,1,0:T(1,128)S(1)} %get-tuple-element.748), channel_id=1, replica_groups=mesh['dp'=2,'seq'=4,'head'=4] {'seq'}, dimensions={0}, use_global_device_ids=true | all-gather | bytes 2560 | tf_op jit(solution)/shard_map/all_gather | solution.py:18
  94.2 14.6 %all_gather.58 = bf16[1024,128]{1,0:T(8,128)(2,1)S(1)} all-gather(bf16[256,128]{1,0:T(8,128)(2,1)S(1)} %copy-done.42), channel_id=1, replica_groups=mesh['dp'=2,'seq'=4,'head'=4] {'seq'}, dimensions={0}, use_global_device_ids=true | all-gather | bytes 327680 | tf_op jit(solution)/shard_map/all_gather | solution.py:116
  109.6 6.8 while.70
  110.3 1.7 fusion.282
  113.7 1.7 fusion.282
  117.1 15.5 %all_gather.59 = bf16[1024,256]{1,0:T(8,128)(2,1)S(1)} all-gather(bf16[256,256]{1,0:T(8,128)(2,1)S(1)} %copy-done.38), channel_id=1, replica_groups=mesh['dp'=2,'seq'=4,'head'=4] {'seq'}, dimensions={0}, use_global_device_ids=true | all-gather | bytes 655360 | tf_op jit(solution)/shard_map/all_gather | solution.py:119
  132.6 14.8 %all_gather.60 = bf16[256,1024]{1,0:T(8,128)(2,1)S(1)} all-gather(bf16[256,256]{1,0:T(8,128)(2,1)S(1)} %copy-done.39), channel_id=1, replica_groups=mesh['dp'=2,'seq'=4,'head'=4] {'seq'}, dimensions={1}, use_global_device_ids=true | all-gather | bytes 655360 | tf_op jit(solution)/shard_map/all_gather | solution.py:121
  151.2 8.8 %all-gather.3 = bf16[4,1,256]{2,1,0:T(2,128)(2,1)S(1)} all-gather(bf16[1,1,256]{2,1,0:T(2,128)(2,1)S(1)} %reshape.779), channel_id=1, replica_groups=mesh['dp'=2,'seq'=4,'head'=4] {'seq'}, dimensions={0}, use_global_device_ids=true | all-gather | bytes 2560 | tf_op jit(solution)/shard_map/all_gather | solution.py:122
  161.1 32.6 %all-reduce.13.cloned.1.call-done = f32[128,1024]{1,0:T(8,128)} async-done(((f32[128,1024]{1,0:T(8,128)}), f32[128,1024]{1,0:T(8,128)}) %all-reduce.13.cloned.1.call-update) | async-done | bytes 524304 | tf_op jit(solution)/shard_map/psum | solution.py:183
  193.7 1.2 multiply_reduce_fusion.3
  195.6 2.7 fusion.132
  198.3 22.5 %all-gather.10.cloned.1.call-done = bf16[1024,704]{0,1:T(8,128)(2,1)} async-done(((bf16[256,704]{0,1:T(8,128)(2,1)}), bf16[1024,704]{0,1:T(8,128)(2,1)}) %all-gather.10.cloned.1.call-update) | async-done | bytes 1441808 | tf_op jit(solution)/shard_map/all_gather | solution.py:124
  220.8 2.6 fusion.133
  223.4 32.5 %all-gather.12.cloned.1.call-done = bf16[704,1024]{1,0:T(8,128)(2,1)} async-done(((bf16[704,256]{1,0:T(8,128)(2,1)}), bf16[704,1024]{1,0:T(8,128)(2,1)}) %all-gather.12.cloned.1.call-update) | async-done | bytes 1441808 | tf_op jit(solution)/shard_map/all_gather | solution.py:125
  255.9 2.2 multiply_convert_fusion.2
  258.8 1.2 convolution_add_fusion.2
  260.9 2.5 convolution_convert_fusion
  263.4 40.4 %all-reduce.17.cloned.1.call-done = f32[128,1024]{1,0:T(8,128)} async-done(((f32[128,1024]{1,0:T(8,128)}), f32[128,1024]{1,0:T(8,128)}) %all-reduce.17.cloned.1.call-update) | async-done | bytes 524304 | tf_op jit(solution)/shard_map/psum | solution.py:203
  303.8 1.8 multiply_reduce_fusion.1
  305.6 44.8 %all-reduce.15.cloned.1.call-done = bf16[128,1024]{1,0:T(8,128)(2,1)} async-done(((bf16[128,1024]{1,0:T(8,128)(2,1)}), bf16[128,1024]{1,0:T(8,128)(2,1)}) %all-reduce.15.cloned.1.call-update) | async-done | bytes 262160 | tf_op jit(solution)/shard_map/psum | solution.py:191
  350.4 2.3 bitcast_add_fusion.7
  352.7 2.6 fusion.94
  355.7 15.3 %all-gather.1 = f32[512,256]{1,0:T(8,128)S(1)} all-gather(f32[128,256]{1,0:T(8,128)S(1)} %fusion.107), channel_id=3, replica_groups=mesh['dp'=2,'seq'=4,'head'=4] {'seq'}, dimensions={0}, use_global_device_ids=true | all-gather | bytes 655360 | tf_op jit(solution)/shard_map/all_gather | solution.py:18
  371.0 2.5 while.69
  374.3 19.5 %while.71 = (s32[]{:T(128)}, f32[1,1,128,256]{2,3,1,0:T(8,128)S(1)}, f32[2,1,1,64,128]{4,3,2,1,0:T(8,128)S(1)}, bf16[2,1,1,64,128]{4,3,2,1,0:T(8,128)(2,1)}, bf1...) while((s32[]{:T(128)}, ...), condition=%wide.region_23.24_spmd.clone.clone, body=%wide.region_16.23_spmd.clone.sunk.clone | while | flops 141848576 | bytes 4776213 | solution.py:76
  376.6 1.3 fusion.300
  378.0 1.2 fusion.298
  379.7 2.3 fusion.303
  386.3 1.3 fusion.300
  387.8 1.2 fusion.298
  389.4 2.3 fusion.303
  395.8 1.8 fusion.137
  397.7 1.4 fusion.95
  399.2 1.3 fusion.138
  400.6 1.3 fusion.139
  402.0 2.1 fusion.140
  405.0 2.1 fusion.141
  408.2 2.1 fusion.124
  412.1 1.1 convolution_add_fusion.5
  413.6 9.2 %psum.158 = bf16[128,16]{0,1:T(8,128)(2,1)S(1)} all-reduce(f32[128,16]{0,1:T(8,128)S(1)} %fusion.111), channel_id=1, replica_groups=mesh['dp'=2,'seq'=4,'head'=4] {'head'}, use_global_device_ids=true, to_apply=%region_25.26 | all-reduce | flops 2048 | bytes 12288 | tf_op jit(solution)/shard_map/psum | solution.py:239
  423.7 15.5 %reduce-scatter.12.cloned.1.call-done = f32[256,128]{1,0:T(8,128)} async-done(((f32[1024,128]{1,0:T(8,128)}), f32[256,128]{1,0:T(8,128)}) %reduce-scatter.12.cloned.1.call-update) | async-done | bytes 131088 | tf_op jit(solution)/shard_map/reduce_scatter | solution.py:249
  439.2 27.9 %reduce-scatter.20.cloned.1.call-done = f32[256,256]{1,0:T(8,128)} async-done(((f32[256,1024]{1,0:T(8,128)}), f32[256,256]{1,0:T(8,128)}) %reduce-scatter.20.cloned.1.call-update) | async-done | bytes 262160 | tf_op jit(solution)/shard_map/reduce_scatter | solution.py:253
  467.1 27.9 %reduce-scatter.14.cloned.1.call-done = f32[256,256]{1,0:T(8,128)} async-done(((f32[1024,256]{1,0:T(8,128)}), f32[256,256]{1,0:T(8,128)}) %reduce-scatter.14.cloned.1.call-update) | async-done | bytes 262160 | tf_op jit(solution)/shard_map/reduce_scatter | solution.py:250
  495.0 27.9 %reduce-scatter.16.cloned.1.call-done = f32[256,256]{1,0:T(8,128)} async-done(((f32[1024,256]{1,0:T(8,128)}), f32[256,256]{1,0:T(8,128)}) %reduce-scatter.16.cloned.1.call-update) | async-done | bytes 262160 | tf_op jit(solution)/shard_map/reduce_scatter | solution.py:251
  522.9 57.0 %reduce-scatter.22.cloned.1.call-done = f32[256,704]{0,1:T(8,128)} async-done(((f32[1024,704]{0,1:T(8,128)}), f32[256,704]{0,1:T(8,128)}) %reduce-scatter.22.cloned.1.call-update) | async-done | bytes 720912 | tf_op jit(solution)/shard_map/reduce_scatter | solution.py:255
  579.9 58.4 %reduce-scatter.24.cloned.1.call-done = f32[256,704]{0,1:T(8,128)} async-done(((f32[1024,704]{0,1:T(8,128)}), f32[256,704]{0,1:T(8,128)}) %reduce-scatter.24.cloned.1.call-update) | async-done | bytes 720912 | tf_op jit(solution)/shard_map/reduce_scatter | solution.py:256
  638.3 58.2 %reduce-scatter.26.cloned.1.call-done = f32[704,256]{1,0:T(8,128)} async-done(((f32[704,1024]{1,0:T(8,128)}), f32[704,256]{1,0:T(8,128)}) %reduce-scatter.26.cloned.1.call-update) | async-done | bytes 720912 | tf_op jit(solution)/shard_map/reduce_scatter | solution.py:257
  698.2 1.4 fusion.84
  699.6 10.3 %all-reduce.4 = (f32[1024]{0:T(1024)S(1)}, f32[1024]{0:T(1024)S(1)}) all-reduce(f32[1024]{0:T(1024)S(1)} %get-tuple-element.643, f32[1024]{0:T(1024)S(1)} %copy-done.43), channel_id=4, replica_groups=mesh['dp'=2,'seq'=4,'head'=4] {'seq'}, use_global_device_ids=true, to_apply=%region_28.29.clone | all-reduce | flops 2048 | bytes 16384
  710.1 8.2 %reduce-scatter.18.cloned.1.call-done = f32[256,16]{0,1:T(8,128)} async-done(((f32[1024,16]{0,1:T(8,128)}), f32[256,16]{0,1:T(8,128)}) %reduce-scatter.18.cloned.1.call-update) | async-done | bytes 16400 | tf_op jit(solution)/shard_map/reduce_scatter | solution.py:252
  718.3 4.8 all-reduce.5
  723.0 74.5 %all-reduce.3 = (f32[16,512]{1,0:T(8,128)}, f32[512]{0:T(512)}, f32[256]{0:T(256)}) all-reduce(f32[16,512]{1,0:T(8,128)S(1)} %get-tuple-element.714, f32[512]{0:T(512)S(1)} %get-tuple-element.715, f32[256]{0:T(256)S(1)} %get-tuple-element.716), channel_id=1, replica_groups=mesh['dp'=2,'seq'=4,'head'=4] {'seq','head'}, use_global_device_ids=true, to_apply=%region_41.42 | all-reduce | flops 8960 | bytes 71680 | tf_op jit(solution)/shard_map/psum | solution.py:293
  798.5 1.7 copy.186
  800.2 1.6 copy.187
  801.8 1.7 copy.188
  803.5 1.7 copy.189
  805.2 1.7 copy.190
  (285 shorter events, 40.0 us)
Async XLA Ops:
  8.0 30.6 %copy-start = (f32[16,512]{1,0:T(8,128)S(1)}, f32[16,512]{1,0:T(8,128)}, u32[]{:S(2)}) copy-start(f32[16,512]{1,0:T(8,128)} %param.32) | copy-start | bytes 98308
  8.0 31.2 %copy-start.37 = (bf16[256,256]{1,0:T(8,128)(2,1)S(1)}, bf16[256,256]{1,0:T(8,128)(2,1)}, u32[]{:S(2)}) copy-start(bf16[256,256]{1,0:T(8,128)(2,1)} %param.29) | copy-start | bytes 393220
  8.0 47.3 %copy-start.41 = (bf16[256,128]{1,0:T(8,128)(2,1)S(1)}, bf16[256,128]{1,0:T(8,128)(2,1)}, u32[]{:S(2)}) copy-start(bf16[256,128]{1,0:T(8,128)(2,1)} %param.28) | copy-start | bytes 196612
  8.0 185.7 %all-reduce.13.cloned.1.call-start = ((), (), s32[]{:S(2)}) async-start(), calls=%async_computation.9 | async-start | bytes 1048576 | tf_op jit(solution)/shard_map/psum | solution.py:183
  9.9 250.8 %copy-start.44 = (f32[128]{0:T(128)}, f32[128]{0:T(128)S(1)}, u32[]{:S(2)}) copy-start(f32[128]{0:T(128)S(1)} %get-tuple-element.750) | copy-start | bytes 1540
  39.0 55.2 %copy-start.24 = (f32[128,128]{1,0:T(8,128)}, f32[128,128]{1,0:T(8,128)S(1)}, u32[]{:S(2)}) copy-start(f32[128,128]{1,0:T(8,128)S(1)} %convolution_add_fusion.7) | copy-start | bytes 196612
  55.4 38.8 %copy-start.42 = (bf16[256,128]{1,0:T(8,128)(2,1)S(1)}, bf16[256,128]{1,0:T(8,128)(2,1)}, u32[]{:S(2)}) copy-start(bf16[256,128]{1,0:T(8,128)(2,1)} %param.27) | copy-start | bytes 196612
  69.9 24.3 %copy-start.7 = (bf16[1024,128]{1,0:T(8,128)(2,1)}, bf16[1024,128]{1,0:T(8,128)(2,1)S(1)}, u32[]{:S(2)}) copy-start(bf16[1024,128]{1,0:T(8,128)(2,1)S(1)} %all_gather.54) | copy-start | bytes 786436
  94.2 15.3 %copy-start.46 = (f32[4,1,1,128]{3,2,1,0:T(1,128)}, f32[4,1,1,128]{3,2,1,0:T(1,128)S(1)}, u32[]{:S(2)}) copy-start(f32[4,1,1,128]{3,2,1,0:T(1,128)S(1)} %get-tuple-element.1290) | copy-start | bytes 6148
  109.1 8.0 copy-start.38
  109.1 23.5 %copy-start.39 = (bf16[256,256]{1,0:T(8,128)(2,1)S(1)}, bf16[256,256]{1,0:T(8,128)(2,1)}, u32[]{:S(2)}) copy-start(bf16[256,256]{1,0:T(8,128)(2,1)} %param.35) | copy-start | bytes 393220
  109.1 38.3 %copy-start.47 = (f32[256]{0:T(256)S(1)}, f32[256]{0:T(256)}, u32[]{:S(2)}) copy-start(f32[256]{0:T(256)} %param.34) | copy-start | bytes 3076
  116.4 33.0 %copy-start.29 = (f32[2,1,1,64,256]{4,3,2,1,0:T(8,128)}, f32[2,1,1,64,256]{4,3,2,1,0:T(8,128)S(1)}, u32[]{:S(2)}) copy-start(f32[2,1,1,64,256]{4,3,2,1,0:T(8,128)S(1)} %get-tuple-element.459) | copy-start | bytes 393220
  117.1 43.5 %copy-start.50 = (f32[128]{0:T(128)}, f32[128]{0:T(128)S(1)}, u32[]{:S(2)}) copy-start(f32[128]{0:T(128)S(1)} %rsqrt.38) | copy-start | bytes 1540
  132.6 17.9 %copy-start.9 = (bf16[1024,256]{1,0:T(8,128)(2,1)}, bf16[1024,256]{1,0:T(8,128)(2,1)S(1)}, u32[]{:S(2)}) copy-start(bf16[1024,256]{1,0:T(8,128)(2,1)S(1)} %all_gather.59) | copy-start | bytes 1572868
  147.4 47.5 %copy-start.11 = (bf16[256,1024]{1,0:T(8,128)(2,1)}, bf16[256,1024]{1,0:T(8,128)(2,1)S(1)}, u32[]{:S(2)}) copy-start(bf16[256,1024]{1,0:T(8,128)(2,1)S(1)} %all_gather.60) | copy-start | bytes 1572868
  147.4 3.8 copy-start.53
  147.4 46.3 %copy-start.1 = (f32[1,128,1024]{2,1,0:T(8,128)S(1)}, f32[1,128,1024]{2,1,0:T(8,128)}, u32[]{:S(2)}) copy-start(f32[1,128,1024]{2,1,0:T(8,128)} %param.24) | copy-start | bytes 1572868
  148.3 12.8 %copy-start.34 = (bf16[128,256]{1,0:T(8,128)(2,1)}, bf16[128,256]{1,0:T(8,128)(2,1)S(1)}, u32[]{:S(2)}) copy-start(bf16[128,256]{1,0:T(8,128)(2,1)S(1)} %get-tuple-element.753) | copy-start | bytes 196612
  149.4 46.2 %all-gather.8.cloned.1.call-start = ((), (), s32[]{:S(2)}) async-start(), calls=%async_computation.10 | async-start | bytes 1802240 | tf_op jit(solution)/shard_map/all_gather | solution.py:123
  149.9 70.9 %all-gather.10.cloned.1.call-start = ((), (), s32[]{:S(2)}) async-start(), calls=%async_computation.11 | async-start | bytes 1802240 | tf_op jit(solution)/shard_map/all_gather | solution.py:124
  150.5 105.4 %all-gather.12.cloned.1.call-start = ((), (), s32[]{:S(2)}) async-start(), calls=%async_computation.12 | async-start | bytes 1802240 | tf_op jit(solution)/shard_map/all_gather | solution.py:125
  151.1 152.7 %all-reduce.17.cloned.1.call-start = ((), (), s32[]{:S(2)}) async-start(), calls=%async_computation.14 | async-start | bytes 1048576 | tf_op jit(solution)/shard_map/psum | solution.py:203
  195.5 60.4 %copy-start.12 = (f32[1,128,1024]{2,1,0:T(8,128)S(1)}, f32[1,128,1024]{2,1,0:T(8,128)}, u32[]{:S(2)}) copy-start(f32[1,128,1024]{2,1,0:T(8,128)} %param.25) | copy-start | bytes 1572868
  255.9 2.3 copy-start.2
  255.9 2.9 copy-start.3
  258.2 1.9 copy-start.20
  258.2 2.7 copy-start.15
  260.1 90.3 %all-reduce.15.cloned.1.call-start = ((), (), s32[]{:S(2)}) async-start(), calls=%async_computation.13 | async-start | bytes 524288 | tf_op jit(solution)/shard_map/psum | solution.py:191
  263.3 89.4 %copy-start.30 = (f32[2,1,1,64,256]{4,3,2,1,0:T(8,128)S(1)}, f32[2,1,1,64,256]{4,3,2,1,0:T(8,128)}, u32[]{:S(2)}) copy-start(f32[2,1,1,64,256]{4,3,2,1,0:T(8,128)} %copy-done.29) | copy-start | bytes 393220
  263.3 89.4 %copy-start.51 = (f32[128]{0:T(128)S(1)}, f32[128]{0:T(128)}, u32[]{:S(2)}) copy-start(f32[128]{0:T(128)} %copy-done.50) | copy-start | bytes 1540
  263.4 160.3 %reduce-scatter.10.cloned.1.call-start = ((), (), s32[]{:S(2)}) async-start(), calls=%async_computation.16 | async-start | bytes 655360 | tf_op jit(solution)/shard_map/reduce_scatter | solution.py:248
  350.4 4.9 copy-start.40
  350.4 4.9 copy-start.52
  355.4 15.6 %copy-start.4 = (f32[128,256]{1,0:T(8,128)}, f32[128,256]{1,0:T(8,128)S(1)}, u32[]{:S(2)}) copy-start(f32[128,256]{1,0:T(8,128)S(1)} %fusion.91) | copy-start | bytes 393220
  374.3 5.0 copy-start.31
  376.6 6.6 copy-start.26
  379.6 4.3 copy-start.32
  384.1 5.0 copy-start.31
  386.3 6.6 copy-start.26
  389.3 4.3 copy-start.32
  393.8 3.9 copy-start.35
  395.8 3.4 copy-start.28
  395.8 43.4 %reduce-scatter.12.cloned.1.call-start = ((), (), s32[]{:S(2)}) async-start(), calls=%async_computation.17 | async-start | bytes 655360 | tf_op jit(solution)/shard_map/reduce_scatter | solution.py:249
  397.7 69.4 %reduce-scatter.20.cloned.1.call-start = ((), (), s32[]{:S(2)}) async-start(), calls=%async_computation.21 | async-start | bytes 1310720 | tf_op jit(solution)/shard_map/reduce_scatter | solution.py:253
  399.1 95.9 %reduce-scatter.14.cloned.1.call-start = ((), (), s32[]{:S(2)}) async-start(), calls=%async_computation.18 | async-start | bytes 1310720 | tf_op jit(solution)/shard_map/reduce_scatter | solution.py:250
  399.2 2.8 copy-start.21
  400.5 122.4 %reduce-scatter.16.cloned.1.call-start = ((), (), s32[]{:S(2)}) async-start(), calls=%async_computation.19 | async-start | bytes 1310720 | tf_op jit(solution)/shard_map/reduce_scatter | solution.py:251
  401.9 178.0 %reduce-scatter.22.cloned.1.call-start = ((), (), s32[]{:S(2)}) async-start(), calls=%async_computation.22 | async-start | bytes 3604480 | tf_op jit(solution)/shard_map/reduce_scatter | solution.py:255
  404.1 234.1 %reduce-scatter.24.cloned.1.call-start = ((), (), s32[]{:S(2)}) async-start(), calls=%async_computation.23 | async-start | bytes 3604480 | tf_op jit(solution)/shard_map/reduce_scatter | solution.py:256
  407.2 289.3 %reduce-scatter.26.cloned.1.call-start = ((), (), s32[]{:S(2)}) async-start(), calls=%async_computation.24 | async-start | bytes 3604480 | tf_op jit(solution)/shard_map/reduce_scatter | solution.py:257
  410.4 1.7 copy-start.10
  410.4 287.8 %all-reduce.19.cloned.1.call-start = ((), (), s32[]{:S(2)}) async-start(), calls=%async_computation.15 | async-start | bytes 1048576 | tf_op jit(solution)/shard_map/psum | solution.py:239
  411.8 1.5 copy-start.25
  413.3 283.2 %copy-start.54 = (u32[32]{0:T(128)S(1)}, u32[32]{0:T(128)}, u32[]{:S(2)}) copy-start(u32[32]{0:T(128)} %constant.207) | copy-start | bytes 388
  413.3 284.9 %copy-start.45 = (f32[128]{0:T(128)S(1)}, f32[128]{0:T(128)}, u32[]{:S(2)}) copy-start(f32[128]{0:T(128)} %copy-done.44) | copy-start | bytes 1540
  413.3 305.0 %reduce-scatter.18.cloned.1.call-start = ((), (), s32[]{:S(2)}) async-start(), calls=%async_computation.20 | async-start | bytes 81920 | tf_op jit(solution)/shard_map/reduce_scatter | solution.py:252
  423.6 374.9 %all-reduce.21.cloned.1.call-start = ((), (), s32[]{:S(2)}) async-start(), calls=%async_computation.25 | async-start | bytes 6422528 | tf_op jit(solution)/shard_map/psum | solution.py:271
  696.5 3.2 copy-start.43
  696.5 21.8 %copy-start.48 = (f32[256]{0:T(256)S(1)}, f32[256]{0:T(256)}, u32[]{:S(2)}) copy-start(f32[256]{0:T(256)} %get-tuple-element.645) | copy-start | bytes 3076
  696.5 101.1 %copy-start.49 = (f32[128]{0:T(128)S(1)}, f32[128]{0:T(128)}, u32[]{:S(2)}) copy-start(f32[128]{0:T(128)} %get-tuple-element.749) | copy-start | bytes 1540
  798.5 8.3 %copy-start.19 = (f32[256,704]{0,1:T(8,128)S(1)}, f32[256,704]{0,1:T(8,128)}, u32[]{:S(2)}) copy-start(f32[256,704]{0,1:T(8,128)} %get-tuple-element.1185) | copy-start | bytes 2162692
  798.5 9.2 %copy-start.18 = (f32[256,704]{0,1:T(8,128)S(1)}, f32[256,704]{0,1:T(8,128)}, u32[]{:S(2)}) copy-start(f32[256,704]{0,1:T(8,128)} %get-tuple-element.1186) | copy-start | bytes 2162692
  801.8 6.8 copy-start.17
  (12 other events, 11.2 us)
Sparse Core Ops, SparseCore 0:
  149.5 44.1 all-reduce.12
  260.2 43.5 all-reduce.16
  307.3 43.0 all-reduce.14
  414.5 43.8 all-reduce.18
  696.6 23.7 all-reduce.20
Sparse Core Ops, SparseCore 1:
  151.4 34.3 all-gather.7
  187.1 33.6 all-gather.9
  222.2 33.6 all-gather.11
  395.8 20.1 reduce-scatter.9
  418.9 20.2 reduce-scatter.11
  441.5 25.5 reduce-scatter.19
  469.2 25.7 reduce-scatter.13
  497.1 25.7 reduce-scatter.15
  525.1 54.8 reduce-scatter.21
  582.2 56.0 reduce-scatter.23
  640.4 56.0 reduce-scatter.25
  699.3 18.9 reduce-scatter.17
